TPU v7x, 512 devices: a whole 4x8x8 slice. The times are simulated.
512 devices in a mesh: orb: 32 (over z, y_lo, core), dom: 16 (over x, y_hi).
Axes of the slice: x: 4, y: 8 (y_hi: 4, y_lo: 2; y = y_hi * 2 + y_lo), z: 8, core: 2. Of those that a mesh axis runs over, the one named last changes fastest.
Arguments:
- orbitals: bfloat16 [32, 16, 192, 128], P('orb', None, 'dom'), may hold values from -6 to 6
- potential: float32 [16, 192, 128], P(None, 'dom'), may hold values from 0 to 2
- degree: int32 [32], P('orb'), may hold values from 1 to 8, as said below
- owners: int32 [4], replicated, may hold values from 0 to 31
- rotation: bfloat16 [4, 1, 32], P(None, None, 'orb'), may hold values from -3 to 3
Outputs:
- filtered: float32 [32, 16, 192, 128], P('orb', None, 'dom')
- rotated: float32 [32, 16, 192, 128], P('orb', None, 'dom')
Inputs may be any that keep to these rules, and one draw needn't show every extreme that they name: Every draw has an orbital of degree 8 and one of degree 1. `owners`: panel numbers; panel q holds orbital q alone.
All inputs are finite; a program needn't handle non-finite values.
Results may differ from a plain program's by a relative error of at most 0.0003.
Values sent between devices are 32-bit elements; how exact they have to be, the bound alone decides.
A program may use at most 64 MiB of HBM per device.

v0:
```python
import jax
import jax.numpy as jnp
from jax import lax
from jax.sharding import PartitionSpec as P

RADIUS = 6
MAXDEG = 8
STEPS = 4


STENCIL = (
    -5369.0 / 1800.0,
    12.0 / 7.0,
    -15.0 / 56.0,
    10.0 / 189.0,
    -1.0 / 112.0,
    2.0 / 1925.0,
    -1.0 / 16632.0,
)
FILTER_CENTER = 7.75
FILTER_HALF = 6.25


def padded_2(block, sides, width):
    for axis, dim in sides:
        count = lax.axis_size(axis)
        forward = [(i, i + 1) for i in range(count - 1)]
        backward = [(target, source) for source, target in forward]
        low = lax.ppermute(
            lax.slice_in_dim(block, block.shape[dim] - width, None, axis=dim), axis, forward
        )
        high = lax.ppermute(lax.slice_in_dim(block, 0, width, axis=dim), axis, backward)
        block = jnp.concatenate([low, block, high], axis=dim)
    return block


def from_root(shard, axis, root):
    mine = lax.axis_index(axis) == root
    return lax.psum(jnp.where(mine, shard, jnp.zeros_like(shard)), axis)


def apply_hamiltonian(padded, potential):
    width = padded.shape[2] - 2 * RADIUS
    center = padded[:, :, RADIUS : RADIUS + width]
    laplace = 3.0 * STENCIL[0] * center
    for offset in range(1, RADIUS + 1):
        beside = (
            padded[:, :, RADIUS + offset : RADIUS + offset + width]
            + padded[:, :, RADIUS - offset : RADIUS - offset + width]
        )
        beside = beside + jnp.roll(center, offset, 3) + jnp.roll(center, -offset, 3)
        beside = beside + jnp.roll(center, offset, 1) + jnp.roll(center, -offset, 1)
        laplace = laplace + STENCIL[offset] * beside
    return -0.5 * laplace + potential * center


def chebyshev_next(applied, current, previous, first):
    shifted = applied - FILTER_CENTER * current
    if first:
        return shifted / FILTER_HALF
    return 2.0 / FILTER_HALF * shifted - previous


def keep_degree(selected, advanced, degree, level):
    return jnp.where((degree == level)[:, None, None, None], advanced, selected)


def per_device(orbitals, potential, degree, owners, rotation):
    block_rows = orbitals.shape[0]
    current = orbitals.astype(jnp.float32)
    previous = current
    selected = jnp.zeros_like(current)
    for section in range(MAXDEG):
        padded = padded_2(current, (("dom", 2),), RADIUS)
        applied = apply_hamiltonian(padded, potential)
        advanced = chebyshev_next(applied, current, previous, section == 0)
        selected = keep_degree(selected, advanced, degree, section + 1)
        previous, current = (current, advanced)
    flattened = selected.reshape(block_rows, -1)
    rotated = jnp.zeros(flattened.shape, jnp.float32)
    for section in range(STEPS):
        panel_block = from_root(flattened, "orb", owners[section])
        coefficients = rotation[section].astype(jnp.float32)
        rotated = rotated + lax.dot_general(
            coefficients,
            panel_block,
            (((0,), (0,)), ((), ())),
            precision=lax.Precision.HIGHEST,
            preferred_element_type=jnp.float32,
        )
    rotated = rotated.reshape(selected.shape)
    return (selected, rotated)


def solution(mesh):
    placed = (
        P("orb", None, "dom", None),
        P(None, "dom", None),
        P("orb"),
        P(),
        P(None, None, "orb"),
    )
    return jax.shard_map(
        per_device,
        mesh=mesh,
        in_specs=placed,
        out_specs=(P("orb", None, "dom", None), P("orb", None, "dom", None)),
        check_vma=False,
    )
```

profile of v0, /device:TPU:7, one launch (start us, length us, event | category | flops | bytes accessed | tf_op | source)
XLA Modules:
  0.0 362.3 jit_solution(5902551951845159628)
XLA Ops:
  7.2 1.4 fusion.652
  8.7 6.1 %collective-permute-start = (f32[1,16,6,128]{3,1,2,0:T(8,128)}, f32[1,16,6,128]{3,1,2,0:T(8,128)}, u32[]{:S(2)}, u32[]{:S(2)}) collective-permute-start(f32[1,16,6,128]{3,1,2,0:T(8,128)} %get-tuple-element.405), channel_id=1, source_target_pairs={{1,0},{2,1},{3,2},{4,3},{5,4},{6,5},{7,6},{8,7},{9,8},{10,9},{11,1... | collective-permute-start | bytes 147464 | tf_op jit(solution)/shard_map/ppermute | solution.py:32
  14.8 1.9 collective-permute-start.1
  27.7 1.8 broadcast_multiply_fusion
  30.9 6.4 %collective-permute-start.2 = (f32[1,16,6,128]{3,1,2,0:T(8,128)S(1)}, f32[1,16,6,128]{3,1,2,0:T(8,128)S(1)}, u32[]{:S(2)}, u32[]{:S(2)}) collective-permute-start(f32[1,16,6,128]{3,1,2,0:T(8,128)S(1)} %get-tuple-element.363), channel_id=1, source_target_pairs={{1,0},{2,1},{3,2},{4,3},{5,4},{6,5},{7,6},{8,7},{9,8},{10,9},{11,1... | collective-permute-start | bytes 147464 | tf_op jit(solution)/shard_map/ppermute | solution.py:32
  37.2 1.9 collective-permute-start.3
  39.2 5.9 %collective-permute-done.3 = f32[1,16,6,128]{3,1,2,0:T(8,128)S(1)} collective-permute-done((f32[1,16,6,128]{3,1,2,0:T(8,128)S(1)}, f32[1,16,6,128]{3,1,2,0:T(8,128)S(1)}, u32[]{:S(2)}, u32[]{:S(2)}) %collective-permute-start.3) | collective-permute-done | bytes 49184 | tf_op jit(solution)/shard_map/ppermute | solution.py:29
  47.1 1.9 collective-permute-start.4
  49.1 4.3 %collective-permute-start.5 = (f32[1,16,6,128]{3,1,2,0:T(8,128)S(1)}, f32[1,16,6,128]{3,1,2,0:T(8,128)S(1)}, u32[]{:S(2)}, u32[]{:S(2)}) collective-permute-start(f32[1,16,6,128]{3,1,2,0:T(8,128)S(1)} %get-tuple-element.314), channel_id=1, source_target_pairs={{0,1},{1,2},{2,3},{3,4},{4,5},{5,6},{6,7},{7,8},{8,9},{9,10},{10,1... | collective-permute-start | bytes 147464 | tf_op jit(solution)/shard_map/ppermute | solution.py:29
  53.4 3.5 collective-permute-done.5
  58.9 1.9 collective-permute-start.6
  60.9 4.3 %collective-permute-start.7 = (f32[1,16,6,128]{3,1,2,0:T(8,128)S(1)}, f32[1,16,6,128]{3,1,2,0:T(8,128)S(1)}, u32[]{:S(2)}, u32[]{:S(2)}) collective-permute-start(f32[1,16,6,128]{3,1,2,0:T(8,128)S(1)} %get-tuple-element.264), channel_id=1, source_target_pairs={{0,1},{1,2},{2,3},{3,4},{4,5},{5,6},{6,7},{7,8},{8,9},{9,10},{10,1... | collective-permute-start | bytes 147464 | tf_op jit(solution)/shard_map/ppermute | solution.py:29
  65.2 3.5 collective-permute-done.7
  70.8 1.9 collective-permute-start.8
  72.7 4.3 %collective-permute-start.9 = (f32[1,16,6,128]{3,1,2,0:T(8,128)S(1)}, f32[1,16,6,128]{3,1,2,0:T(8,128)S(1)}, u32[]{:S(2)}, u32[]{:S(2)}) collective-permute-start(f32[1,16,6,128]{3,1,2,0:T(8,128)S(1)} %get-tuple-element.214), channel_id=1, source_target_pairs={{0,1},{1,2},{2,3},{3,4},{4,5},{5,6},{6,7},{7,8},{8,9},{9,10},{10,1... | collective-permute-start | bytes 147464 | tf_op jit(solution)/shard_map/ppermute | solution.py:29
  77.0 3.7 %collective-permute-done.9 = f32[1,16,6,128]{3,1,2,0:T(8,128)S(1)} collective-permute-done((f32[1,16,6,128]{3,1,2,0:T(8,128)S(1)}, f32[1,16,6,128]{3,1,2,0:T(8,128)S(1)}, u32[]{:S(2)}, u32[]{:S(2)}) %collective-permute-start.9) | collective-permute-done | bytes 49184 | tf_op jit(solution)/shard_map/ppermute | solution.py:29
  82.8 2.8 collective-permute-start.10
  85.6 3.4 collective-permute-start.11
  89.0 4.4 %collective-permute-done.11 = f32[1,16,6,128]{3,1,2,0:T(8,128)S(1)} collective-permute-done((f32[1,16,6,128]{3,1,2,0:T(8,128)S(1)}, f32[1,16,6,128]{3,1,2,0:T(8,128)S(1)}, u32[]{:S(2)}, u32[]{:S(2)}) %collective-permute-start.11) | collective-permute-done | bytes 49184 | tf_op jit(solution)/shard_map/ppermute | solution.py:29
  95.5 1.9 collective-permute-start.12
  97.4 4.3 %collective-permute-start.13 = (f32[1,16,6,128]{3,1,2,0:T(8,128)S(1)}, f32[1,16,6,128]{3,1,2,0:T(8,128)S(1)}, u32[]{:S(2)}, u32[]{:S(2)}) collective-permute-start(f32[1,16,6,128]{3,1,2,0:T(8,128)S(1)} %get-tuple-element.114), channel_id=1, source_target_pairs={{0,1},{1,2},{2,3},{3,4},{4,5},{5,6},{6,7},{7,8},{8,9},{9,10},{10,1... | collective-permute-start | bytes 147464 | tf_op jit(solution)/shard_map/ppermute | solution.py:29
  101.7 3.5 collective-permute-done.13
  107.3 1.9 collective-permute-start.14
  109.2 4.3 %collective-permute-start.15 = (f32[1,16,6,128]{3,1,2,0:T(8,128)S(1)}, f32[1,16,6,128]{3,1,2,0:T(8,128)S(1)}, u32[]{:S(2)}, u32[]{:S(2)}) collective-permute-start(f32[1,16,6,128]{3,1,2,0:T(8,128)S(1)} %get-tuple-element.56), channel_id=1, source_target_pairs={{0,1},{1,2},{2,3},{3,4},{4,5},{5,6},{6,7},{7,8},{8,9},{9,10},{10,1... | collective-permute-start | bytes 147464 | tf_op jit(solution)/shard_map/ppermute | solution.py:29
  113.6 3.4 collective-permute-done.15
  117.1 0.7 broadcast_select_fusion.3
  118.5 0.7 select_n.108
  119.3 0.7 select_n.111
  120.1 0.7 select_n.114
  120.8 0.7 select_n.105
  124.7 228.6 %all-reduce.3.cloned.1.call-done = (f32[1,24576]{1,0:T(1,128)}, f32[1,24576]{1,0:T(1,128)}, f32[1,24576]{1,0:T(1,128)}, f32[1,24576]{1,0:T(1,128)}) async-done(((f32[1,24576]{1,0:T(1,128)}, f32[1,24576]{1,0:T(1,128)}, f32[1,24576]{1,0:T(1,128)}, f32[1,24576]{1,0:T(1,128)}), (f32[1,24576]{1,0:T(1,128)}, f32[1,24576]{1,0:T(1,128)}, f32[1,24576]{1,0:T(1,128)}, ...) | async-done | bytes 393232 | tf_op jit(solution)/shard_map/psum | solution.py:39
  353.3 1.4 add_reduce_fusion
  (242 shorter events, 22.5 us)
Async XLA Ops:
  7.2 346.1 %all-reduce.3.cloned.1.call-start = ((), (), s32[]{:S(2)}) async-start(), calls=%async_computation | async-start | bytes 786432 | tf_op jit(solution)/shard_map/psum | solution.py:39
  7.2 9.5 %copy-start = (bf16[1,16,12,128]{3,1,2,0:T(8,128)(2,1)S(1)}, bf16[1,16,12,128]{3,1,2,0:T(8,128)(2,1)}, u32[]{:S(2)}) copy-start(bf16[1,16,12,128]{3,1,2,0:T(8,128)(2,1)} %param.5) | copy-start | bytes 147460
  8.7 18.3 %collective-permute-start = (f32[1,16,6,128]{3,1,2,0:T(8,128)}, f32[1,16,6,128]{3,1,2,0:T(8,128)}, u32[]{:S(2)}, u32[]{:S(2)}) collective-permute-start(f32[1,16,6,128]{3,1,2,0:T(8,128)} %get-tuple-element.405), channel_id=1, source_target_pairs={{1,0},{2,1},{3,2},{4,3},{5,4},{6,5},{7,6},{8,7},{9,8},{10,9},{11,1... | collective-permute-start | bytes 147464 | tf_op jit(solution)/shard_map/ppermute | solution.py:32
  14.8 12.2 %collective-permute-start.1 = (f32[1,16,6,128]{3,1,2,0:T(8,128)}, f32[1,16,6,128]{3,1,2,0:T(8,128)}, u32[]{:S(2)}, u32[]{:S(2)}) collective-permute-start(f32[1,16,6,128]{3,1,2,0:T(8,128)} %get-tuple-element.406), channel_id=1, source_target_pairs={{0,1},{1,2},{2,3},{3,4},{4,5},{5,6},{6,7},{7,8},{8,9},{9,10},{10,1... | collective-permute-start | bytes 147464 | tf_op jit(solution)/shard_map/ppermute | solution.py:29
  21.2 1.8 copy-start.6
  23.7 3.3 copy-start.1
  27.0 0.7 copy-start.3
  27.0 0.7 copy-start.4
  27.0 0.7 copy-start.5
  30.9 8.3 %collective-permute-start.2 = (f32[1,16,6,128]{3,1,2,0:T(8,128)S(1)}, f32[1,16,6,128]{3,1,2,0:T(8,128)S(1)}, u32[]{:S(2)}, u32[]{:S(2)}) collective-permute-start(f32[1,16,6,128]{3,1,2,0:T(8,128)S(1)} %get-tuple-element.363), channel_id=1, source_target_pairs={{1,0},{2,1},{3,2},{4,3},{5,4},{6,5},{7,6},{8,7},{9,8},{10,9},{11,1... | collective-permute-start | bytes 147464 | tf_op jit(solution)/shard_map/ppermute | solution.py:32
  37.2 7.8 %collective-permute-start.3 = (f32[1,16,6,128]{3,1,2,0:T(8,128)S(1)}, f32[1,16,6,128]{3,1,2,0:T(8,128)S(1)}, u32[]{:S(2)}, u32[]{:S(2)}) collective-permute-start(f32[1,16,6,128]{3,1,2,0:T(8,128)S(1)} %get-tuple-element.364), channel_id=1, source_target_pairs={{0,1},{1,2},{2,3},{3,4},{4,5},{5,6},{6,7},{7,8},{8,9},{9,10},{10,1... | collective-permute-start | bytes 147464 | tf_op jit(solution)/shard_map/ppermute | solution.py:29
  47.1 6.3 %collective-permute-start.4 = (f32[1,16,6,128]{3,1,2,0:T(8,128)S(1)}, f32[1,16,6,128]{3,1,2,0:T(8,128)S(1)}, u32[]{:S(2)}, u32[]{:S(2)}) collective-permute-start(f32[1,16,6,128]{3,1,2,0:T(8,128)S(1)} %get-tuple-element.313), channel_id=1, source_target_pairs={{1,0},{2,1},{3,2},{4,3},{5,4},{6,5},{7,6},{8,7},{9,8},{10,9},{11,1... | collective-permute-start | bytes 147464 | tf_op jit(solution)/shard_map/ppermute | solution.py:32
  49.1 7.8 %collective-permute-start.5 = (f32[1,16,6,128]{3,1,2,0:T(8,128)S(1)}, f32[1,16,6,128]{3,1,2,0:T(8,128)S(1)}, u32[]{:S(2)}, u32[]{:S(2)}) collective-permute-start(f32[1,16,6,128]{3,1,2,0:T(8,128)S(1)} %get-tuple-element.314), channel_id=1, source_target_pairs={{0,1},{1,2},{2,3},{3,4},{4,5},{5,6},{6,7},{7,8},{8,9},{9,10},{10,1... | collective-permute-start | bytes 147464 | tf_op jit(solution)/shard_map/ppermute | solution.py:29
  58.9 6.3 %collective-permute-start.6 = (f32[1,16,6,128]{3,1,2,0:T(8,128)S(1)}, f32[1,16,6,128]{3,1,2,0:T(8,128)S(1)}, u32[]{:S(2)}, u32[]{:S(2)}) collective-permute-start(f32[1,16,6,128]{3,1,2,0:T(8,128)S(1)} %get-tuple-element.263), channel_id=1, source_target_pairs={{1,0},{2,1},{3,2},{4,3},{5,4},{6,5},{7,6},{8,7},{9,8},{10,9},{11,1... | collective-permute-start | bytes 147464 | tf_op jit(solution)/shard_map/ppermute | solution.py:32
  60.9 7.8 %collective-permute-start.7 = (f32[1,16,6,128]{3,1,2,0:T(8,128)S(1)}, f32[1,16,6,128]{3,1,2,0:T(8,128)S(1)}, u32[]{:S(2)}, u32[]{:S(2)}) collective-permute-start(f32[1,16,6,128]{3,1,2,0:T(8,128)S(1)} %get-tuple-element.264), channel_id=1, source_target_pairs={{0,1},{1,2},{2,3},{3,4},{4,5},{5,6},{6,7},{7,8},{8,9},{9,10},{10,1... | collective-permute-start | bytes 147464 | tf_op jit(solution)/shard_map/ppermute | solution.py:29
  70.8 6.3 %collective-permute-start.8 = (f32[1,16,6,128]{3,1,2,0:T(8,128)S(1)}, f32[1,16,6,128]{3,1,2,0:T(8,128)S(1)}, u32[]{:S(2)}, u32[]{:S(2)}) collective-permute-start(f32[1,16,6,128]{3,1,2,0:T(8,128)S(1)} %get-tuple-element.213), channel_id=1, source_target_pairs={{1,0},{2,1},{3,2},{4,3},{5,4},{6,5},{7,6},{8,7},{9,8},{10,9},{11,1... | collective-permute-start | bytes 147464 | tf_op jit(solution)/shard_map/ppermute | solution.py:32
  72.7 8.1 %collective-permute-start.9 = (f32[1,16,6,128]{3,1,2,0:T(8,128)S(1)}, f32[1,16,6,128]{3,1,2,0:T(8,128)S(1)}, u32[]{:S(2)}, u32[]{:S(2)}) collective-permute-start(f32[1,16,6,128]{3,1,2,0:T(8,128)S(1)} %get-tuple-element.214), channel_id=1, source_target_pairs={{0,1},{1,2},{2,3},{3,4},{4,5},{5,6},{6,7},{7,8},{8,9},{9,10},{10,1... | collective-permute-start | bytes 147464 | tf_op jit(solution)/shard_map/ppermute | solution.py:29
  82.8 6.2 %collective-permute-start.10 = (f32[1,16,6,128]{3,1,2,0:T(8,128)S(1)}, f32[1,16,6,128]{3,1,2,0:T(8,128)S(1)}, u32[]{:S(2)}, u32[]{:S(2)}) collective-permute-start(f32[1,16,6,128]{3,1,2,0:T(8,128)S(1)} %get-tuple-element.163), channel_id=1, source_target_pairs={{1,0},{2,1},{3,2},{4,3},{5,4},{6,5},{7,6},{8,7},{9,8},{10,9},{11,1... | collective-permute-start | bytes 147464 | tf_op jit(solution)/shard_map/ppermute | solution.py:32
  85.6 7.8 %collective-permute-start.11 = (f32[1,16,6,128]{3,1,2,0:T(8,128)S(1)}, f32[1,16,6,128]{3,1,2,0:T(8,128)S(1)}, u32[]{:S(2)}, u32[]{:S(2)}) collective-permute-start(f32[1,16,6,128]{3,1,2,0:T(8,128)S(1)} %get-tuple-element.164), channel_id=1, source_target_pairs={{0,1},{1,2},{2,3},{3,4},{4,5},{5,6},{6,7},{7,8},{8,9},{9,10},{10,1... | collective-permute-start | bytes 147464 | tf_op jit(solution)/shard_map/ppermute | solution.py:29
  95.5 6.2 %collective-permute-start.12 = (f32[1,16,6,128]{3,1,2,0:T(8,128)S(1)}, f32[1,16,6,128]{3,1,2,0:T(8,128)S(1)}, u32[]{:S(2)}, u32[]{:S(2)}) collective-permute-start(f32[1,16,6,128]{3,1,2,0:T(8,128)S(1)} %get-tuple-element.113), channel_id=1, source_target_pairs={{1,0},{2,1},{3,2},{4,3},{5,4},{6,5},{7,6},{8,7},{9,8},{10,9},{11,1... | collective-permute-start | bytes 147464 | tf_op jit(solution)/shard_map/ppermute | solution.py:32
  97.4 7.8 %collective-permute-start.13 = (f32[1,16,6,128]{3,1,2,0:T(8,128)S(1)}, f32[1,16,6,128]{3,1,2,0:T(8,128)S(1)}, u32[]{:S(2)}, u32[]{:S(2)}) collective-permute-start(f32[1,16,6,128]{3,1,2,0:T(8,128)S(1)} %get-tuple-element.114), channel_id=1, source_target_pairs={{0,1},{1,2},{2,3},{3,4},{4,5},{5,6},{6,7},{7,8},{8,9},{9,10},{10,1... | collective-permute-start | bytes 147464 | tf_op jit(solution)/shard_map/ppermute | solution.py:29
  107.3 6.3 %collective-permute-start.14 = (f32[1,16,6,128]{3,1,2,0:T(8,128)S(1)}, f32[1,16,6,128]{3,1,2,0:T(8,128)S(1)}, u32[]{:S(2)}, u32[]{:S(2)}) collective-permute-start(f32[1,16,6,128]{3,1,2,0:T(8,128)S(1)} %get-tuple-element.55), channel_id=1, source_target_pairs={{1,0},{2,1},{3,2},{4,3},{5,4},{6,5},{7,6},{8,7},{9,8},{10,9},{11,1... | collective-permute-start | bytes 147464 | tf_op jit(solution)/shard_map/ppermute | solution.py:32
  109.2 7.8 %collective-permute-start.15 = (f32[1,16,6,128]{3,1,2,0:T(8,128)S(1)}, f32[1,16,6,128]{3,1,2,0:T(8,128)S(1)}, u32[]{:S(2)}, u32[]{:S(2)}) collective-permute-start(f32[1,16,6,128]{3,1,2,0:T(8,128)S(1)} %get-tuple-element.56), channel_id=1, source_target_pairs={{0,1},{1,2},{2,3},{3,4},{4,5},{5,6},{6,7},{7,8},{8,9},{9,10},{10,1... | collective-permute-start | bytes 147464 | tf_op jit(solution)/shard_map/ppermute | solution.py:29
  117.8 0.6 copy-start.2
  120.0 1.5 copy-start.7
Sparse Core Ops, SparseCore 0:
  121.7 231.5 all-reduce.2
where the time goes:
time: 364 us; the launch traced here: 362 us
  waiting for transfers between devices  257 us (71%)
  starting transfers between devices  53.5 us (15%)
  local copies, waits for them, and re-layouts  22.4 us (6%)
  between operations  21.4 us (6%)
  other arithmetic  8.01 us (2%)
    psum x1, waiting for transfers between devices, from_root(): return lax.psum(jnp.where(mine, shard, jnp.zeros_like(shard)), axis)  229 us
    ppermute x8, starting transfers between devices, padded_2(): lax.ppermute(lax.slice_in_dim(block, block.shape[dim] - width, None, axis...  28.5 us
    ppermute x8, waiting for transfers between devices, padded_2(): lax.ppermute(lax.slice_in_dim(block, block.shape[dim] - width, None, axis...  28 us
    ppermute x8, starting transfers between devices, padded_2(): lax.ppermute(lax.slice_in_dim(block, 0, width, axis=dim), axis, backward)  24.9 us
    slice x96, local copies, waits for them, and re-layouts, apply_hamiltonian(): beside = beside + jnp.roll(center, offset, 3) + jnp.roll(center, -offset, 3)  8.87 us
  transfers between devices with their start and end apart: 17, of which 10 were waited for; matrix products, arithmetic and copies ran while one was open for 2% of the time, Pallas kernels for 0%

commit v1 on v0

v1 whole, which is shorter than its diff:
```python
import jax
import jax.numpy as jnp
import numpy as np
from jax import lax
from jax.experimental import pallas as pl
from jax.experimental.pallas import tpu as pltpu
from jax.sharding import PartitionSpec as P

RADIUS = 6
MAXDEG = 8
STEPS = 4
ROUNDS = 4
STENCIL = (
    -5369.0 / 1800.0,
    12.0 / 7.0,
    -15.0 / 56.0,
    10.0 / 189.0,
    -1.0 / 112.0,
    2.0 / 1925.0,
    -1.0 / 16632.0,
)
FILTER_CENTER = 7.75
FILTER_HALF = 6.25
SCALE = 2.0 / FILTER_HALF
MESH = pl.DeviceIdType.MESH

SIDE = [-0.5 * SCALE * c for c in STENCIL]
CENTRE = 3.0 * SIDE[0] - SCALE * FILTER_CENTER


def circulant(size):
    matrix = np.zeros((size, size), np.float64)
    for offset in range(1, RADIUS + 1):
        for index in range(size):
            matrix[index, (index + offset) % size] += SIDE[offset]
            matrix[index, (index - offset) % size] += SIDE[offset]
    return matrix


def halves(matrix):
    high = matrix.astype(jnp.bfloat16)
    low = (matrix - high.astype(np.float64)).astype(jnp.bfloat16)
    return high, low


def stencil_matrices(planes, cells, layers):
    high, low = halves(circulant(cells))
    along_y = np.block([[high, low], [high, low]])
    high, low = halves(np.kron(np.eye(layers), circulant(planes)))
    along_p = np.block([[high, high], [low, low]])
    return along_y, along_p


def filter_kernel(width, orb_ref, pot_ref, degree_ref, ymat_ref, pmat_ref, out_ref,
                  field, inner, diag, send_sem, recv_sem, pot_send, pot_recv):
    count = lax.axis_size("dom")
    me = lax.axis_index("dom")
    has_left = me > 0
    has_right = me < count - 1
    half = RADIUS
    w = width

    def to_left(src, dst, ssem, rsem):
        return pltpu.make_async_remote_copy(
            src_ref=src, dst_ref=dst, send_sem=ssem, recv_sem=rsem,
            device_id={"dom": jnp.maximum(me - 1, 0)}, device_id_type=MESH)

    def to_right(src, dst, ssem, rsem):
        return pltpu.make_async_remote_copy(
            src_ref=src, dst_ref=dst, send_sem=ssem, recv_sem=rsem,
            device_id={"dom": jnp.minimum(me + 1, count - 1)}, device_id_type=MESH)

    def copies(r):
        src = orb_ref if r == 0 else field.at[r, pl.ds(w, w)]
        left = to_left(src, field.at[r, pl.ds(2 * w, w)], send_sem.at[r, 0], recv_sem.at[r, 0])
        right = to_right(src, field.at[r, pl.ds(0, w)], send_sem.at[r, 1], recv_sem.at[r, 1])
        return left, right

    pot_left = to_left(pot_ref.at[pl.ds(0, half)], diag.at[pl.ds(half + w, half)], pot_send.at[0], pot_recv.at[0])
    pot_right = to_right(pot_ref.at[pl.ds(w - half, half)], diag.at[pl.ds(0, half)], pot_send.at[1], pot_recv.at[1])

    barrier = pltpu.get_barrier_semaphore()

    for shift in (1, count - 1):
        pl.semaphore_signal(
            barrier, inc=1, device_id={"dom": lax.rem(me + shift, count)}, device_id_type=MESH)
    pl.semaphore_wait(barrier, 2)

    def start(r):
        left, right = copies(r)

        @pl.when(has_left)
        def _():
            left.start()
            if r == 0:
                pot_left.start()

        @pl.when(has_right)
        def _():
            right.start()
            if r == 0:
                pot_right.start()

    def arrive(r):
        left, right = copies(r)

        @pl.when(has_left)
        def _():
            right.wait_recv()
            if r == 0:
                pot_right.wait_recv()

        @pl.when(has_right)
        def _():
            left.wait_recv()
            if r == 0:
                pot_left.wait_recv()

    start(0)

    @pl.when(jnp.logical_not(has_left))
    def _():
        for r in range(ROUNDS):
            field[r, 0:w] = jnp.zeros((w,) + field.shape[2:], jnp.float32)
        diag[0:half] = jnp.zeros((half,) + diag.shape[1:], jnp.float32)

    @pl.when(jnp.logical_not(has_right))
    def _():
        for r in range(ROUNDS):
            field[r, 2 * w:3 * w] = jnp.zeros((w,) + field.shape[2:], jnp.float32)
        diag[half + w:2 * half + w] = jnp.zeros((half,) + diag.shape[1:], jnp.float32)

    field[0, w:2 * w] = orb_ref[...]
    diag[half:half + w] = pot_ref[...]

    planes, cells = field.shape[2], field.shape[3]
    rows = half * planes
    left_mask = jnp.where(has_left, 1.0, 0.0).astype(jnp.float32)
    right_mask = jnp.where(has_right, 1.0, 0.0).astype(jnp.float32)
    degree = degree_ref[0]

    def applied(ref, low, diag_low):
        centre = ref[pl.ds(low, w)]
        total = (diag[pl.ds(diag_low, w)] * SCALE + CENTRE) * centre
        for offset in range(1, RADIUS + 1):
            total = total + SIDE[offset] * (ref[pl.ds(low + offset, w)] + ref[pl.ds(low - offset, w)])
        flat = centre.reshape(2 * rows, cells)
        high = flat.astype(jnp.bfloat16)
        rest = (flat - high.astype(jnp.float32)).astype(jnp.bfloat16)
        both = jnp.dot(jnp.concatenate([high, rest], axis=1), ymat_ref[...], preferred_element_type=jnp.float32)
        total = total + (both[:, :cells] + both[:, cells:]).reshape(centre.shape)
        stacked = jnp.concatenate([
            jnp.concatenate([high[:rows], high[rows:]], axis=1),
            jnp.concatenate([rest[:rows], rest[rows:]], axis=1)], axis=0)
        both = jnp.dot(pmat_ref[...], stacked, preferred_element_type=jnp.float32)
        both = both[:rows] + both[rows:]
        both = jnp.concatenate([both[:, :cells], both[:, cells:]], axis=0)
        return total + both.reshape(centre.shape)

    for r in range(ROUNDS):
        arrive(r)
        now = field.at[r]
        for part in range(2):
            low = part * w
            advanced = applied(now, low + half, low)
            if r == 0:
                advanced = 0.5 * advanced
            else:
                advanced = advanced - inner[low:low + w]
            if part == 0:
                inner[0:half] = advanced[:half] * left_mask
                inner[half:w] = advanced[half:]
            else:
                inner[w:w + half] = advanced[:half]
                inner[w + half:2 * w] = advanced[half:] * right_mask
        advanced = applied(inner, half, half) - now[w:2 * w]
        if r + 1 < ROUNDS:
            field[r + 1, w:2 * w] = advanced
            start(r + 1)
        before = out_ref[...] if r > 0 else jnp.zeros_like(advanced)
        before = jnp.where(degree == 2 * r + 1, inner[half:half + w], before)
        out_ref[...] = jnp.where(degree == 2 * r + 2, advanced, before)

    @pl.when(has_left)
    def _():
        for r in range(ROUNDS):
            copies(r)[0].wait_send()
        pot_left.wait_send()

    @pl.when(has_right)
    def _():
        for r in range(ROUNDS):
            copies(r)[1].wait_send()
        pot_right.wait_send()


def filtered_layers(orbitals, potential, degree):
    width, planes, cells = orbitals.shape
    ymat, pmat = stencil_matrices(planes, cells, RADIUS)
    vmem = pl.BlockSpec(memory_space=pltpu.VMEM)
    smem = pl.BlockSpec(memory_space=pltpu.SMEM)
    return pl.pallas_call(
        lambda *refs: filter_kernel(width, *refs),
        out_shape=jax.ShapeDtypeStruct(orbitals.shape, jnp.float32),
        in_specs=[vmem, vmem, smem, vmem, vmem],
        out_specs=vmem,
        scratch_shapes=[
            pltpu.VMEM((ROUNDS, 3 * width, planes, cells), jnp.float32),
            pltpu.VMEM((2 * width, planes, cells), jnp.float32),
            pltpu.VMEM((width + 2 * RADIUS, planes, cells), jnp.float32),
            pltpu.SemaphoreType.DMA((ROUNDS, 2)),
            pltpu.SemaphoreType.DMA((ROUNDS, 2)),
            pltpu.SemaphoreType.DMA((2,)),
            pltpu.SemaphoreType.DMA((2,)),
        ],
        compiler_params=pltpu.CompilerParams(collective_id=0, has_side_effects=True),
        name="chebyshev",
    )(orbitals, potential, degree, jnp.asarray(ymat), jnp.asarray(pmat))


def from_root(shard, axis, root):
    mine = lax.axis_index(axis) == root
    return lax.psum(jnp.where(mine, shard, jnp.zeros_like(shard)), axis)


def per_device(orbitals, potential, degree, owners, rotation):
    layers = jnp.transpose(orbitals[0].astype(jnp.float32), (1, 0, 2))
    selected = filtered_layers(layers, jnp.transpose(potential, (1, 0, 2)), degree)
    selected = jnp.transpose(selected, (1, 0, 2))[None]
    rotated = jnp.zeros(selected.shape, jnp.float32)
    for section in range(STEPS):
        panel = from_root(selected, "orb", owners[section])
        rotated = rotated + rotation[section, 0, 0].astype(jnp.float32) * panel
    return (selected, rotated)


def solution(mesh):
    placed = (
        P("orb", None, "dom", None),
        P(None, "dom", None),
        P("orb"),
        P(),
        P(None, None, "orb"),
    )
    return jax.shard_map(
        per_device,
        mesh=mesh,
        in_specs=placed,
        out_specs=(P("orb", None, "dom", None), P("orb", None, "dom", None)),
        check_vma=False,
    )
```

time: 364 us -> 284 us (0.78)
  starting transfers between devices: 53.5 us -> 0.04 us
  waiting for transfers between devices: 257 us -> 221 us
  Pallas kernels: 0 us -> 34.2 us
  local copies, waits for them, and re-layouts: 22.4 us -> 3.18 us
    ppermute x16 -> x0, starting transfers between devices: 53.4 us -> none  [the longest x8 28.5 us: padded_2(): lax.ppermute(lax.slice_in_dim(block, block.shape[dim] - width, None, axis...]
    pallas_call x0 -> x1, Pallas kernels: none -> 34.2 us  [filtered_layers(): pl.pallas_call(lambda *refs: filter_kernel(width, *refs), out_shape=jax.S...]
    ppermute x16 -> x0, waiting for transfers between devices: 28.3 us -> none  [the longest x8 28 us: padded_2(): lax.ppermute(lax.slice_in_dim(block, block.shape[dim] - width, None, axis...]
    slice x202 -> x2, local copies, waits for them, and re-layouts: 17.3 us -> 1.3 us  [the longest x1 0.66 us: per_device(): panel = from_root(selected, 'orb', owners[section])]
    psum x1, waiting for transfers between devices: 229 us -> 221 us  [from_root(): return lax.psum(jnp.where(mine, shard, jnp.zeros_like(shard)), axis)]
    sub x6 -> x0, other arithmetic: 4.04 us -> none  [chebyshev_next(): return 2.0 / FILTER_HALF * shifted - previous]
  transfers between devices with their start and end apart: 17 -> 1, of which waited for: 10 -> 1; matrix products, arithmetic and copies ran while one was open for 2% -> 0% of each run, Pallas kernels for 0% -> 0%
where the time goes in v1:
time: 284 us; the launch traced here: 283 us
  waiting for transfers between devices  221 us (78%)
  Pallas kernels  34.2 us (12%)
  between operations  19.8 us (7%)
  other arithmetic  4.81 us (2%)
  local copies, waits for them, and re-layouts  3.18 us (1%)
    psum x1, waiting for transfers between devices, from_root(): return lax.psum(jnp.where(mine, shard, jnp.zeros_like(shard)), axis)  221 us
    pallas_call x1, Pallas kernels, filtered_layers(): pl.pallas_call(lambda *refs: filter_kernel(width, *refs), out_shape=jax.S...  34.2 us
  transfers between devices with their start and end apart: 1, of which 1 were waited for; matrix products, arithmetic and copies ran while one was open for 0% of the time, Pallas kernels for 0%

profile of v1, /device:TPU:7, one launch (start us, length us, event | category | flops | bytes accessed | tf_op | source)
XLA Modules:
  0.0 282.5 jit_solution(8609933765789078702)
XLA Ops:
  7.2 0.0 copy-start.1
  7.2 0.0 all-reduce.3.cloned.1.call-start
  7.2 0.6 copy-done.1
  7.8 0.7 fusion.5
  11.1 1.4 convert_bitcast_fusion.refs_0_
  13.2 34.2 %chebyshev.1 = f32[12,16,128]{2,1,0:T(8,128)} custom-call(f32[12,16,128]{2,1,0:T(8,128)} %convert_bitcast_fusion.refs_0_, f32[12,16,128]{2,1,0:T(8,128)} %bitcast.42, s32[1]{0:T(128)S(6)} %copy.14.refs_2_, bf16[256,256]{1,0:T(8,128)(2,1)} %constant.12.clone.refs_3_, bf16[192,192]{1,0:T(8,128)(2,1)} %constant.13.clone.refs_4_), custom_call_target="tpu_custom_call" | custom-call | tf_op jit(solution)/shard_map/chebyshev/pallas_call | solution.py:202
  47.4 1.6 fusion.1
  49.1 0.0 copy-start.2
  49.1 0.0 all-reduce.3.cloned.1.call-update
  49.1 0.6 copy-done.2
  49.7 0.6 fusion.4
  52.8 220.5 %all-reduce.3.cloned.1.call-done = (f32[1,16,12,128]{3,1,2,0:T(8,128)}, f32[1,16,12,128]{3,1,2,0:T(8,128)}, f32[1,16,12,128]{3,1,2,0:T(8,128)}, f32[1,16,12,128]{3,1,2,0:T(8,128)}) async-done(((f32[1,16,12,128]{3,1,2,0:T(8,128)}, f32[1,16,12,128]{3,1,2,0:T(8,128)}, f32[1,16,12,128]{3,1,2,0:T(8,128)}, f32[1,16,12,128]{3,1,2,0:T(8,128)}), (f32[1,16,12,128]{3,1,2,0:T(8,128)}, f32[1,16,12,128]{3,1,2,0:T(8,128)}, ...) | async-done | bytes 393232 | tf_op jit(solution)/shard_map/psum | solution.py:223
  273.3 0.0 copy-start
  273.3 1.7 multiply_add_fusion
  275.0 0.0 copy-done
  275.1 0.6 copy.15
Async XLA Ops:
  7.2 0.7 copy-start.1
  7.2 266.1 %all-reduce.3.cloned.1.call-start = ((), (), s32[]{:S(2)}) async-start(), calls=%async_computation | async-start | bytes 786432 | tf_op jit(solution)/shard_map/psum | solution.py:223
  49.1 0.7 copy-start.2
  273.3 1.7 copy-start
Sparse Core Ops, SparseCore 0:
  49.2 224.0 all-reduce.2

commit v2 on v1

--- a/solution.py
+++ b/solution.py
@@ -51,8 +51,141 @@
     return along_y, along_p
 
 
-def filter_kernel(width, orb_ref, pot_ref, degree_ref, ymat_ref, pmat_ref, out_ref,
-                  field, inner, diag, send_sem, recv_sem, pot_send, pot_recv):
+def seat():
+    orb = lax.axis_index("orb")
+    return orb // 4, lax.rem(orb // 2, 2), lax.rem(orb, 2)
+
+
+def at(z, pair, core):
+    return {"orb": z * 4 + pair * 2 + core}
+
+
+def by_distance(chips):
+    return sorted(range(1, chips), key=lambda step: (min(step, chips - step), step))
+
+
+def rotation_peers():
+    chips = lax.axis_size("orb") // 4
+    z, pair, core = seat()
+    return [at(z, pair, 1 - core), at(z, 1 - pair, core)] + [
+        at(lax.rem(z + step, chips), pair, core) for step in by_distance(chips)]
+
+
+def rotate(filtered, owner_ref, rot_ref, rotated_ref, own, give, got_core, give_pair, got_pair,
+           give_z, got_z, panels, sems):
+    chips = lax.axis_size("orb") // 4
+    z, pair, core = seat()
+    orb = lax.axis_index("orb")
+    near = by_distance(chips)
+    chunk_of = lambda step: lax.rem(z + step, chips)
+    mate, across = at(z, pair, 1 - core), at(z, 1 - pair, core)
+
+    def copy(stage, src, dst, slot, peer, landing=None):
+        return pltpu.make_async_remote_copy(
+            src_ref=src, dst_ref=dst, send_sem=sems.at[stage, 0, slot],
+            recv_sem=sems.at[stage, 1, slot if landing is None else landing],
+            device_id=peer, device_id_type=MESH)
+
+    def to_mate(k):
+        return copy(0, give.at[:, k], got_core.at[:, k], k, mate)
+
+    def to_across(k):
+        return copy(1, give_pair.at[k], got_pair.at[k], k, across)
+
+    def scatter(k):
+        return copy(2, give_z.at[k], got_z.at[z], k, at(k, pair, core), z)
+
+    def scattered(k):
+        return copy(2, give_z.at[k], got_z.at[k], k, at(k, pair, core))
+
+    def gather(k):
+        piece = panels.at[core, pair, z]
+        return copy(3, piece, piece, k, at(k, pair, core), z)
+
+    def gathered(k):
+        piece = panels.at[core, pair, k]
+        return copy(3, piece, piece, k, at(k, pair, core))
+
+    def share_across(k):
+        piece = panels.at[core, pair, k]
+        return copy(4, piece, piece, k, across)
+
+    def shared_across(k):
+        piece = panels.at[core, 1 - pair, k]
+        return copy(4, piece, piece, k, across)
+
+    def share_mate(k, which):
+        piece = panels.at[core, which, k]
+        return copy(5, piece, piece, which * chips + k, mate)
+
+    def shared_mate(k, which):
+        piece = panels.at[1 - core, which, k]
+        return copy(5, piece, piece, which * chips + k, mate)
+
+    own[...] = filtered.reshape(own.shape)
+
+    def masked(panel, k):
+        return jnp.where(owner_ref[panel] == orb, own[k], 0.0)
+
+    far_first = near[::-1] + [0]
+    for step in far_first:
+        k = chunk_of(step)
+        for which in range(2):
+            give[which, k] = masked(2 * which + 1 - core, k)
+        to_mate(k).start()
+    for step in far_first:
+        k = chunk_of(step)
+        to_mate(k).wait_recv()
+        give_pair[k] = got_core[1 - pair, k] + masked(2 * (1 - pair) + core, k)
+        to_across(k).start()
+    for step in far_first:
+        k = chunk_of(step)
+        to_across(k).wait_recv()
+        part = got_core[pair, k] + masked(2 * pair + core, k) + got_pair[k]
+        if step == 0:
+            got_z[z] = part
+        else:
+            give_z[k] = part
+            scatter(k).start()
+    for step in near:
+        scattered(chunk_of(step)).wait_recv()
+    total = got_z[0]
+    for k in range(1, chips):
+        total = total + got_z[k]
+    panels[core, pair, z] = total
+    for step in near[::-1]:
+        gather(chunk_of(step)).start()
+    for step in [0] + near:
+        k = chunk_of(step)
+        if step != 0:
+            gathered(k).wait_recv()
+        share_across(k).start()
+        share_mate(k, pair).start()
+    for step in [0] + near:
+        k = chunk_of(step)
+        shared_across(k).wait_recv()
+        share_mate(k, 1 - pair).start()
+    for step in [0] + near:
+        k = chunk_of(step)
+        shared_mate(k, pair).wait_recv()
+        shared_mate(k, 1 - pair).wait_recv()
+        rotated_ref[k] = (rot_ref[0] * panels[0, 0, k] + rot_ref[1] * panels[1, 0, k]
+                          + rot_ref[2] * panels[0, 1, k] + rot_ref[3] * panels[1, 1, k])
+    for step in [0] + near:
+        k = chunk_of(step)
+        to_mate(k).wait_send()
+        to_across(k).wait_send()
+        if step != 0:
+            scatter(k).wait_send()
+            gather(k).wait_send()
+        share_across(k).wait_send()
+        share_mate(k, pair).wait_send()
+        share_mate(k, 1 - pair).wait_send()
+
+
+def filter_kernel(width, orb_ref, pot_ref, degree_ref, owner_ref, rot_ref, ymat_ref, pmat_ref,
+                  out_ref, rotated_ref, field, inner, diag, send_sem, recv_sem, pot_send, pot_recv,
+                  *rotation_scratch):
     count = lax.axis_size("dom")
     me = lax.axis_index("dom")
     has_left = me > 0
@@ -81,10 +214,10 @@
 
     barrier = pltpu.get_barrier_semaphore()
 
-    for shift in (1, count - 1):
-        pl.semaphore_signal(
-            barrier, inc=1, device_id={"dom": lax.rem(me + shift, count)}, device_id_type=MESH)
-    pl.semaphore_wait(barrier, 2)
+    peers = [{"dom": lax.rem(me + shift, count)} for shift in (1, count - 1)] + rotation_peers()
+    for peer in peers:
+        pl.semaphore_signal(barrier, inc=1, device_id=peer, device_id_type=MESH)
+    pl.semaphore_wait(barrier, len(peers))
 
     def start(r):
         left, right = copies(r)
@@ -181,6 +314,8 @@
         before = jnp.where(degree == 2 * r + 1, inner[half:half + w], before)
         out_ref[...] = jnp.where(degree == 2 * r + 2, advanced, before)
 
+    rotate(out_ref[...], owner_ref, rot_ref, rotated_ref, *rotation_scratch)
+
     @pl.when(has_left)
     def _():
         for r in range(ROUNDS):
@@ -194,16 +329,22 @@
         pot_right.wait_send()
 
 
-def filtered_layers(orbitals, potential, degree):
+def filter_and_rotate(orbitals, potential, degree, owners, coefficients):
     width, planes, cells = orbitals.shape
+    chips = lax.axis_size("orb") // 4
+    piece = (width * planes // 8 // chips, 8, cells)
     ymat, pmat = stencil_matrices(planes, cells, RADIUS)
     vmem = pl.BlockSpec(memory_space=pltpu.VMEM)
     smem = pl.BlockSpec(memory_space=pltpu.SMEM)
-    return pl.pallas_call(
+    buffer = lambda *lead: pltpu.VMEM(lead + piece, jnp.float32)
+    filtered, rotated = pl.pallas_call(
         lambda *refs: filter_kernel(width, *refs),
-        out_shape=jax.ShapeDtypeStruct(orbitals.shape, jnp.float32),
-        in_specs=[vmem, vmem, smem, vmem, vmem],
-        out_specs=vmem,
+        out_shape=(
+            jax.ShapeDtypeStruct(orbitals.shape, jnp.float32),
+            jax.ShapeDtypeStruct((chips,) + piece, jnp.float32),
+        ),
+        in_specs=[vmem, vmem, smem, smem, smem, vmem, vmem],
+        out_specs=(vmem, vmem),
         scratch_shapes=[
             pltpu.VMEM((ROUNDS, 3 * width, planes, cells), jnp.float32),
             pltpu.VMEM((2 * width, planes, cells), jnp.float32),
@@ -212,26 +353,22 @@
             pltpu.SemaphoreType.DMA((ROUNDS, 2)),
             pltpu.SemaphoreType.DMA((2,)),
             pltpu.SemaphoreType.DMA((2,)),
+            buffer(chips), buffer(2, chips), buffer(2, chips), buffer(chips), buffer(chips),
+            buffer(chips), buffer(chips), buffer(2, 2, chips),
+            pltpu.SemaphoreType.DMA((6, 2, 2 * chips)),
         ],
         compiler_params=pltpu.CompilerParams(collective_id=0, has_side_effects=True),
-        name="chebyshev",
-    )(orbitals, potential, degree, jnp.asarray(ymat), jnp.asarray(pmat))
-
-
-def from_root(shard, axis, root):
-    mine = lax.axis_index(axis) == root
-    return lax.psum(jnp.where(mine, shard, jnp.zeros_like(shard)), axis)
+        name="filter_rotate",
+    )(orbitals, potential, degree, owners, coefficients, jnp.asarray(ymat), jnp.asarray(pmat))
+    return filtered, rotated.reshape(orbitals.shape)
 
 
 def per_device(orbitals, potential, degree, owners, rotation):
     layers = jnp.transpose(orbitals[0].astype(jnp.float32), (1, 0, 2))
-    selected = filtered_layers(layers, jnp.transpose(potential, (1, 0, 2)), degree)
-    selected = jnp.transpose(selected, (1, 0, 2))[None]
-    rotated = jnp.zeros(selected.shape, jnp.float32)
-    for section in range(STEPS):
-        panel = from_root(selected, "orb", owners[section])
-        rotated = rotated + rotation[section, 0, 0].astype(jnp.float32) * panel
-    return (selected, rotated)
+    filtered, rotated = filter_and_rotate(
+        layers, jnp.transpose(potential, (1, 0, 2)), degree, owners,
+        rotation.astype(jnp.float32).reshape(STEPS))
+    return jnp.transpose(filtered, (1, 0, 2))[None], jnp.transpose(rotated, (1, 0, 2))[None]
 
 
 def solution(mesh):

time: 284 us -> 70.2 us (0.25)
  waiting for transfers between devices: 221 us -> 0 us
  Pallas kernels: 34.2 us -> 63.9 us
  between operations: 19.8 us -> 1.3 us
  other arithmetic: 4.81 us -> 1.96 us
    psum x1 -> x0, waiting for transfers between devices: 221 us -> none  [from_root(): return lax.psum(jnp.where(mine, shard, jnp.zeros_like(shard)), axis)]
    pallas_call x1, Pallas kernels: 34.2 us -> 63.9 us  [filter_and_rotate(): pl.pallas_call(lambda *refs: filter_kernel(width, *refs), out_shape=(jax....]
  transfers between devices with their start and end apart: 1 -> 0, of which waited for: 1 -> 0; matrix products, arithmetic and copies ran while one was open for 0% -> 0% of each run, Pallas kernels for 0% -> 0%
where the time goes in v2:
time: 70.2 us; the launch traced here: 70 us
  Pallas kernels  63.9 us (91%)
  local copies, waits for them, and re-layouts  2.87 us (4%)
  other arithmetic  1.96 us (3%)
  between operations  1.3 us (2%)
    pallas_call x1, Pallas kernels, filter_and_rotate(): pl.pallas_call(lambda *refs: filter_kernel(width, *refs), out_shape=(jax....  63.9 us
    unnamed x6, local copies, waits for them, and re-layouts  2.87 us
    transpose x1, other arithmetic, per_device(): layers = jnp.transpose(orbitals[0].astype(jnp.float32), (1, 0, 2))  1.45 us

profile of v2, /device:TPU:7, one launch (start us, length us, event | category | flops | bytes accessed | tf_op | source)
XLA Modules:
  0.0 70.0 jit_solution(14817914164753716812)
XLA Ops:
  1.3 0.0 copy-start.1
  1.3 0.6 copy-done.1
  1.9 0.5 bitcast_convert_fusion.refs_4_
  2.4 1.4 %convert_bitcast_fusion.refs_0_ = f32[12,16,128]{2,1,0:T(8,128)} fusion(bf16[1,16,12,128]{3,1,2,0:T(8,128)(2,1)} %param.7), kind=kLoop, calls=%fused_computation | loop fusion | flops 24576 | bytes 147456 | tf_op jit(solution)/shard_map/transpose | solution.py:367
  3.9 63.9 %filter_rotate.1 = (f32[12,16,128]{2,1,0:T(8,128)}, f32[8,3,8,128]{3,2,1,0:T(8,128)}) custom-call(f32[12,16,128]{2,1,0:T(8,128)} %convert_bitcast_fusion.refs_0_, f32[12,16,128]{2,1,0:T(8,128)} %bitcast.19, s32[1]{0:T(128)S(6)} %copy.11.refs_2_, s32[4]{0:T(128)} %refs_3_.1, f32[4]{0:T(128)} %bitcast_convert_fusion.refs_4_, ...), custom_call_target="tpu_custom_call" | custom-call | tf_op jit(solution)/shard_map/filter_rotate/pallas_call | solution.py:340
  67.8 0.0 copy-start
  67.8 1.6 %copy.12 = f32[1,16,12,128]{3,1,2,0:T(8,128)} copy(f32[1,16,12,128]{3,1,2,0:T(8,128)} %bitcast.18) | data formatting | bytes 196608
  69.3 0.0 copy-done
  69.3 0.6 copy.13
Async XLA Ops:
  1.3 0.7 copy-start.1
  67.8 1.6 %copy-start = (f32[8,3,8,128]{3,2,1,0:T(8,128)S(1)}, f32[8,3,8,128]{3,2,1,0:T(8,128)}, u32[]{:S(2)}) copy-start(f32[8,3,8,128]{3,2,1,0:T(8,128)} %get-tuple-element.5) | copy-start | bytes 294916

commit v3 on v2

--- a/solution.py
+++ b/solution.py
@@ -123,6 +123,9 @@
         return copy(5, piece, piece, which * chips + k, mate)
 
     own[...] = filtered.reshape(own.shape)
+    row = rot_ref[...].astype(jnp.float32)
+    lane = lax.broadcasted_iota(jnp.int32, row.shape, 1)
+    weight = [jnp.sum(jnp.where(lane == panel, row, 0.0), axis=1, keepdims=True)[None] for panel in range(STEPS)]
 
     def masked(panel, k):
         return jnp.where(owner_ref[panel] == orb, own[k], 0.0)
@@ -169,8 +172,8 @@
         k = chunk_of(step)
         shared_mate(k, pair).wait_recv()
         shared_mate(k, 1 - pair).wait_recv()
-        rotated_ref[k] = (rot_ref[0] * panels[0, 0, k] + rot_ref[1] * panels[1, 0, k]
-                          + rot_ref[2] * panels[0, 1, k] + rot_ref[3] * panels[1, 1, k])
+        rotated_ref[k] = (weight[0] * panels[0, 0, k] + weight[1] * panels[1, 0, k]
+                          + weight[2] * panels[0, 1, k] + weight[3] * panels[1, 1, k])
     for step in [0] + near:
         k = chunk_of(step)
         to_mate(k).wait_send()
@@ -185,7 +188,7 @@
 
 def filter_kernel(width, orb_ref, pot_ref, degree_ref, owner_ref, rot_ref, ymat_ref, pmat_ref,
                   out_ref, rotated_ref, field, inner, diag, send_sem, recv_sem, pot_send, pot_recv,
-                  *rotation_scratch):
+                  hand_send, hand_recv, go_sem, *rotation_scratch):
     count = lax.axis_size("dom")
     me = lax.axis_index("dom")
     has_left = me > 0
@@ -204,52 +207,62 @@
             device_id={"dom": jnp.minimum(me + 1, count - 1)}, device_id_type=MESH)
 
     def copies(r):
-        src = orb_ref if r == 0 else field.at[r, pl.ds(w, w)]
+        src = field.at[r, pl.ds(w, w)]
         left = to_left(src, field.at[r, pl.ds(2 * w, w)], send_sem.at[r, 0], recv_sem.at[r, 0])
         right = to_right(src, field.at[r, pl.ds(0, w)], send_sem.at[r, 1], recv_sem.at[r, 1])
         return left, right
 
-    pot_left = to_left(pot_ref.at[pl.ds(0, half)], diag.at[pl.ds(half + w, half)], pot_send.at[0], pot_recv.at[0])
-    pot_right = to_right(pot_ref.at[pl.ds(w - half, half)], diag.at[pl.ds(0, half)], pot_send.at[1], pot_recv.at[1])
-
+    z, pair, core = seat()
+    mate = at(z, pair, 1 - core)
+    is_first = core == 0
+    is_second = core == 1
+    low_half, high_half = pl.ds(0, half), pl.ds(half + w, half)
+    pot_left = lambda: to_left(pot_ref.at[pl.ds(0, half)], diag.at[high_half], pot_send.at[0], pot_recv.at[0])
+    pot_right = lambda: to_right(pot_ref.at[pl.ds(w - half, half)], diag.at[low_half], pot_send.at[1], pot_recv.at[1])
+
+    def hand(side):
+        part = diag.at[high_half if side else low_half]
+        return pltpu.make_async_remote_copy(
+            src_ref=part, dst_ref=part, send_sem=hand_send.at[side], recv_sem=hand_recv.at[side],
+            device_id=mate, device_id_type=MESH)
+
+    def on(condition, *actions):
+        @pl.when(condition)
+        def _():
+            for action in actions:
+                action()
+
+    peers = [{"dom": lax.rem(me + shift, count)} for shift in (1, count - 1)] + rotation_peers()
     barrier = pltpu.get_barrier_semaphore()
-
-    peers = [{"dom": lax.rem(me + shift, count)} for shift in (1, count - 1)] + rotation_peers()
     for peer in peers:
         pl.semaphore_signal(barrier, inc=1, device_id=peer, device_id_type=MESH)
+    field[0, w:2 * w] = orb_ref[...].astype(jnp.float32)
     pl.semaphore_wait(barrier, len(peers))
 
     def start(r):
-        left, right = copies(r)
-
-        @pl.when(has_left)
-        def _():
-            left.start()
-            if r == 0:
-                pot_left.start()
-
-        @pl.when(has_right)
-        def _():
-            right.start()
-            if r == 0:
-                pot_right.start()
+        on(has_left, lambda: copies(r)[0].start())
+        on(has_right, lambda: copies(r)[1].start())
+
+    def sent(r):
+        on(has_left, lambda: copies(r)[0].wait_send())
+        on(has_right, lambda: copies(r)[1].wait_send())
 
     def arrive(r):
-        left, right = copies(r)
-
-        @pl.when(has_left)
-        def _():
-            right.wait_recv()
-            if r == 0:
-                pot_right.wait_recv()
-
-        @pl.when(has_right)
-        def _():
-            left.wait_recv()
-            if r == 0:
-                pot_left.wait_recv()
-
-    start(0)
+        on(has_left, lambda: copies(r)[1].wait_recv())
+        on(has_right, lambda: copies(r)[0].wait_recv())
+
+    @pl.when(is_first)
+    def _():
+        start(0)
+        sent(0)
+        pl.semaphore_signal(go_sem, inc=1, device_id=mate, device_id_type=MESH)
+
+    @pl.when(is_second)
+    def _():
+        on(has_left, lambda: pot_left().start())
+        on(has_right, lambda: pot_right().start())
+        pl.semaphore_wait(go_sem, 1)
+        start(0)
 
     @pl.when(jnp.logical_not(has_left))
     def _():
@@ -263,8 +276,17 @@
             field[r, 2 * w:3 * w] = jnp.zeros((w,) + field.shape[2:], jnp.float32)
         diag[half + w:2 * half + w] = jnp.zeros((half,) + diag.shape[1:], jnp.float32)
 
-    field[0, w:2 * w] = orb_ref[...]
     diag[half:half + w] = pot_ref[...]
+
+    @pl.when(is_second)
+    def _():
+        on(has_left, lambda: pot_right().wait_recv(), lambda: hand(0).start())
+        on(has_right, lambda: pot_left().wait_recv(), lambda: hand(1).start())
+
+    @pl.when(is_first)
+    def _():
+        on(has_left, lambda: hand(0).wait_recv())
+        on(has_right, lambda: hand(1).wait_recv())
 
     planes, cells = field.shape[2], field.shape[3]
     rows = half * planes
@@ -316,17 +338,14 @@
 
     rotate(out_ref[...], owner_ref, rot_ref, rotated_ref, *rotation_scratch)
 
-    @pl.when(has_left)
-    def _():
-        for r in range(ROUNDS):
-            copies(r)[0].wait_send()
-        pot_left.wait_send()
-
-    @pl.when(has_right)
-    def _():
-        for r in range(ROUNDS):
-            copies(r)[1].wait_send()
-        pot_right.wait_send()
+    for r in range(1, ROUNDS):
+        sent(r)
+
+    @pl.when(is_second)
+    def _():
+        sent(0)
+        on(has_left, lambda: pot_left().wait_send(), lambda: hand(0).wait_send())
+        on(has_right, lambda: pot_right().wait_send(), lambda: hand(1).wait_send())
 
 
 def filter_and_rotate(orbitals, potential, degree, owners, coefficients):
@@ -343,7 +362,7 @@
             jax.ShapeDtypeStruct(orbitals.shape, jnp.float32),
             jax.ShapeDtypeStruct((chips,) + piece, jnp.float32),
         ),
-        in_specs=[vmem, vmem, smem, smem, smem, vmem, vmem],
+        in_specs=[vmem, vmem, smem, smem, vmem, vmem, vmem],
         out_specs=(vmem, vmem),
         scratch_shapes=[
             pltpu.VMEM((ROUNDS, 3 * width, planes, cells), jnp.float32),
@@ -353,6 +372,9 @@
             pltpu.SemaphoreType.DMA((ROUNDS, 2)),
             pltpu.SemaphoreType.DMA((2,)),
             pltpu.SemaphoreType.DMA((2,)),
+            pltpu.SemaphoreType.DMA((2,)),
+            pltpu.SemaphoreType.DMA((2,)),
+            pltpu.SemaphoreType.REGULAR,
             buffer(chips), buffer(2, chips), buffer(2, chips), buffer(chips), buffer(chips),
             buffer(chips), buffer(chips), buffer(2, 2, chips),
             pltpu.SemaphoreType.DMA((6, 2, 2 * chips)),
@@ -364,10 +386,10 @@
 
 
 def per_device(orbitals, potential, degree, owners, rotation):
-    layers = jnp.transpose(orbitals[0].astype(jnp.float32), (1, 0, 2))
+    layers = jnp.transpose(orbitals[0], (1, 0, 2))
     filtered, rotated = filter_and_rotate(
         layers, jnp.transpose(potential, (1, 0, 2)), degree, owners,
-        rotation.astype(jnp.float32).reshape(STEPS))
+        rotation.reshape(1, STEPS))
     return jnp.transpose(filtered, (1, 0, 2))[None], jnp.transpose(rotated, (1, 0, 2))[None]
 
 

time: 70.2 us -> 66.4 us (0.946)
  other arithmetic: 1.96 us -> 0 us
  Pallas kernels: 63.9 us -> 62.8 us
    transpose x1 -> x0, other arithmetic: 1.45 us -> none  [per_device(): layers = jnp.transpose(orbitals[0].astype(jnp.float32), (1, 0, 2))]
    pallas_call x1, Pallas kernels: 63.9 us -> 62.8 us  [filter_and_rotate(): pl.pallas_call(lambda *refs: filter_kernel(width, *refs), out_shape=(jax....]
    unnamed x6 -> x4, local copies, waits for them, and re-layouts: 2.87 us -> 2.22 us
where the time goes in v3:
time: 66.4 us; the launch traced here: 66.3 us
  Pallas kernels  62.8 us (95%)
  local copies, waits for them, and re-layouts  2.22 us (3%)
  between operations  1.29 us (2%)
    pallas_call x1, Pallas kernels, filter_and_rotate(): pl.pallas_call(lambda *refs: filter_kernel(width, *refs), out_shape=(jax....  62.8 us
    unnamed x4, local copies, waits for them, and re-layouts  2.22 us

profile of v3, /device:TPU:7, one launch (start us, length us, event | category | flops | bytes accessed | tf_op | source)
XLA Modules:
  0.0 66.3 jit_solution(18403696173638291968)
XLA Ops:
  1.3 62.8 %filter_rotate.1 = (f32[12,16,128]{2,1,0:T(8,128)}, f32[8,3,8,128]{3,2,1,0:T(8,128)}) custom-call(bf16[12,16,128]{2,1,0:T(8,128)(2,1)} %bitcast.16, f32[12,16,128]{2,1,0:T(8,128)} %bitcast.15, s32[1]{0:T(128)S(6)} %copy.11.refs_2_, s32[4]{0:T(128)} %refs_3_.1, bf16[1,4]{1,0:T(2,128)(2,1)} %bitcast.17, bf16[256,256]{1,0:T(8,128)(2,1)} %constant.4.clone.refs_5_, ...), custom_call_target="tpu_custom_call" | custom-call | tf_op jit(solution)/shard_map/filter_rotate/pallas_call | solution.py:359
  64.0 0.0 copy-start
  64.1 1.6 %copy.12 = f32[1,16,12,128]{3,1,2,0:T(8,128)} copy(f32[1,16,12,128]{3,1,2,0:T(8,128)} %bitcast.14) | data formatting | bytes 196608
  65.6 0.0 copy-done
  65.6 0.6 copy.13
Async XLA Ops:
  64.0 1.6 %copy-start = (f32[8,3,8,128]{3,2,1,0:T(8,128)S(1)}, f32[8,3,8,128]{3,2,1,0:T(8,128)}, u32[]{:S(2)}) copy-start(f32[8,3,8,128]{3,2,1,0:T(8,128)} %get-tuple-element.5) | copy-start | bytes 294916

commit v4 on v3

--- a/solution.py
+++ b/solution.py
@@ -71,8 +71,8 @@
         at(lax.rem(z + step, chips), pair, core) for step in by_distance(chips)]
 
 
-def rotate(filtered, owner_ref, rot_ref, rotated_ref, own, give, got_core, give_pair, got_pair,
-           give_z, got_z, panels, sems):
+def rotate(filtered, owner_ref, rot_ref, rotated_ref, own, give, got_core, give_z, got_z, give_pair,
+           got_pair, panels, sems):
     chips = lax.axis_size("orb") // 4
     z, pair, core = seat()
     orb = lax.axis_index("orb")
@@ -87,40 +87,32 @@
             device_id=peer, device_id_type=MESH)
 
     def to_mate(k):
-        return copy(0, give.at[:, k], got_core.at[:, k], k, mate)
-
-    def to_across(k):
-        return copy(1, give_pair.at[k], got_pair.at[k], k, across)
+        return copy(0, give.at[k], got_core.at[k], k, mate)
 
     def scatter(k):
-        return copy(2, give_z.at[k], got_z.at[z], k, at(k, pair, core), z)
+        return copy(1, give_z.at[k], got_z.at[z], k, at(k, pair, core), z)
 
     def scattered(k):
-        return copy(2, give_z.at[k], got_z.at[k], k, at(k, pair, core))
+        return copy(1, give_z.at[k], got_z.at[k], k, at(k, pair, core))
+
+    def to_across():
+        return copy(2, give_pair, got_pair, 0, across)
 
     def gather(k):
-        piece = panels.at[core, pair, z]
+        piece = panels.at[core, z]
         return copy(3, piece, piece, k, at(k, pair, core), z)
 
     def gathered(k):
-        piece = panels.at[core, pair, k]
+        piece = panels.at[core, k]
         return copy(3, piece, piece, k, at(k, pair, core))
 
-    def share_across(k):
-        piece = panels.at[core, pair, k]
-        return copy(4, piece, piece, k, across)
-
-    def shared_across(k):
-        piece = panels.at[core, 1 - pair, k]
-        return copy(4, piece, piece, k, across)
-
-    def share_mate(k, which):
-        piece = panels.at[core, which, k]
-        return copy(5, piece, piece, which * chips + k, mate)
-
-    def shared_mate(k, which):
-        piece = panels.at[1 - core, which, k]
-        return copy(5, piece, piece, which * chips + k, mate)
+    def share(k):
+        piece = panels.at[core, k]
+        return copy(4, piece, piece, k, mate)
+
+    def shared(k):
+        piece = panels.at[1 - core, k]
+        return copy(4, piece, piece, k, mate)
 
     own[...] = filtered.reshape(own.shape)
     row = rot_ref[...].astype(jnp.float32)
@@ -134,56 +126,45 @@
     for step in far_first:
         k = chunk_of(step)
         for which in range(2):
-            give[which, k] = masked(2 * which + 1 - core, k)
+            give[k, which] = masked(2 * which + 1 - core, k)
         to_mate(k).start()
     for step in far_first:
         k = chunk_of(step)
         to_mate(k).wait_recv()
-        give_pair[k] = got_core[1 - pair, k] + masked(2 * (1 - pair) + core, k)
-        to_across(k).start()
-    for step in far_first:
-        k = chunk_of(step)
-        to_across(k).wait_recv()
-        part = got_core[pair, k] + masked(2 * pair + core, k) + got_pair[k]
-        if step == 0:
-            got_z[z] = part
-        else:
-            give_z[k] = part
+        target = got_z if step == 0 else give_z
+        for which in range(2):
+            target[k, which] = got_core[k, which] + masked(2 * which + core, k)
+        if step != 0:
             scatter(k).start()
     for step in near:
         scattered(chunk_of(step)).wait_recv()
     total = got_z[0]
     for k in range(1, chips):
         total = total + got_z[k]
-    panels[core, pair, z] = total
+    give_pair[...] = total
+    to_across().start()
+    to_across().wait_recv()
+    panels[core, z] = give_pair[...] + got_pair[...]
     for step in near[::-1]:
         gather(chunk_of(step)).start()
     for step in [0] + near:
         k = chunk_of(step)
         if step != 0:
             gathered(k).wait_recv()
-        share_across(k).start()
-        share_mate(k, pair).start()
+        share(k).start()
     for step in [0] + near:
         k = chunk_of(step)
-        shared_across(k).wait_recv()
-        share_mate(k, 1 - pair).start()
+        shared(k).wait_recv()
+        rotated_ref[k] = (weight[0] * panels[0, k, 0] + weight[1] * panels[1, k, 0]
+                          + weight[2] * panels[0, k, 1] + weight[3] * panels[1, k, 1])
     for step in [0] + near:
         k = chunk_of(step)
-        shared_mate(k, pair).wait_recv()
-        shared_mate(k, 1 - pair).wait_recv()
-        rotated_ref[k] = (weight[0] * panels[0, 0, k] + weight[1] * panels[1, 0, k]
-                          + weight[2] * panels[0, 1, k] + weight[3] * panels[1, 1, k])
-    for step in [0] + near:
-        k = chunk_of(step)
         to_mate(k).wait_send()
-        to_across(k).wait_send()
         if step != 0:
             scatter(k).wait_send()
             gather(k).wait_send()
-        share_across(k).wait_send()
-        share_mate(k, pair).wait_send()
-        share_mate(k, 1 - pair).wait_send()
+        share(k).wait_send()
+    to_across().wait_send()
 
 
 def filter_kernel(width, orb_ref, pot_ref, degree_ref, owner_ref, rot_ref, ymat_ref, pmat_ref,
@@ -294,41 +275,42 @@
     right_mask = jnp.where(has_right, 1.0, 0.0).astype(jnp.float32)
     degree = degree_ref[0]
 
-    def applied(ref, low, diag_low):
-        centre = ref[pl.ds(low, w)]
-        total = (diag[pl.ds(diag_low, w)] * SCALE + CENTRE) * centre
-        for offset in range(1, RADIUS + 1):
-            total = total + SIDE[offset] * (ref[pl.ds(low + offset, w)] + ref[pl.ds(low - offset, w)])
+    def along_yp(centre):
         flat = centre.reshape(2 * rows, cells)
         high = flat.astype(jnp.bfloat16)
         rest = (flat - high.astype(jnp.float32)).astype(jnp.bfloat16)
         both = jnp.dot(jnp.concatenate([high, rest], axis=1), ymat_ref[...], preferred_element_type=jnp.float32)
-        total = total + (both[:, :cells] + both[:, cells:]).reshape(centre.shape)
+        total = both[:, :cells] + both[:, cells:]
         stacked = jnp.concatenate([
             jnp.concatenate([high[:rows], high[rows:]], axis=1),
             jnp.concatenate([rest[:rows], rest[rows:]], axis=1)], axis=0)
         both = jnp.dot(pmat_ref[...], stacked, preferred_element_type=jnp.float32)
         both = both[:rows] + both[rows:]
         both = jnp.concatenate([both[:, :cells], both[:, cells:]], axis=0)
-        return total + both.reshape(centre.shape)
+        return (total + both).reshape(centre.shape)
+
+    def along_x(ref, low, diag_low, layers):
+        total = (diag[diag_low:diag_low + layers] * SCALE + CENTRE) * ref[low:low + layers]
+        for offset in range(1, RADIUS + 1):
+            total = total + SIDE[offset] * (
+                ref[low + offset:low + offset + layers] + ref[low - offset:low - offset + layers])
+        return total
 
     for r in range(ROUNDS):
+        now = field.at[r]
+        own_part = along_yp(now[w:2 * w])
         arrive(r)
-        now = field.at[r]
-        for part in range(2):
-            low = part * w
-            advanced = applied(now, low + half, low)
-            if r == 0:
-                advanced = 0.5 * advanced
-            else:
-                advanced = advanced - inner[low:low + w]
-            if part == 0:
-                inner[0:half] = advanced[:half] * left_mask
-                inner[half:w] = advanced[half:]
-            else:
-                inner[w:w + half] = advanced[:half]
-                inner[w + half:2 * w] = advanced[half:] * right_mask
-        advanced = applied(inner, half, half) - now[w:2 * w]
+        halo_part = along_yp(jnp.concatenate([now[w - half:w], now[2 * w:2 * w + half]], axis=0))
+        strips = (
+            (0, half, halo_part[:half], left_mask),
+            (half, w, own_part, None),
+            (half + w, half, halo_part[half:], right_mask),
+        )
+        for low, layers, part, mask in strips:
+            advanced = along_x(now, low + half, low, layers) + part
+            advanced = 0.5 * advanced if r == 0 else advanced - inner[low:low + layers]
+            inner[low:low + layers] = advanced if mask is None else advanced * mask
+        advanced = along_x(inner, half, half, w) + along_yp(inner[half:half + w]) - now[w:2 * w]
         if r + 1 < ROUNDS:
             field[r + 1, w:2 * w] = advanced
             start(r + 1)
@@ -359,8 +341,8 @@
     filtered, rotated = pl.pallas_call(
         lambda *refs: filter_kernel(width, *refs),
         out_shape=(
-            jax.ShapeDtypeStruct(orbitals.shape, jnp.float32),
-            jax.ShapeDtypeStruct((chips,) + piece, jnp.float32),
+            pltpu.VMEM(orbitals.shape, jnp.float32),
+            pltpu.VMEM((chips,) + piece, jnp.float32),
         ),
         in_specs=[vmem, vmem, smem, smem, vmem, vmem, vmem],
         out_specs=(vmem, vmem),
@@ -375,9 +357,9 @@
             pltpu.SemaphoreType.DMA((2,)),
             pltpu.SemaphoreType.DMA((2,)),
             pltpu.SemaphoreType.REGULAR,
-            buffer(chips), buffer(2, chips), buffer(2, chips), buffer(chips), buffer(chips),
-            buffer(chips), buffer(chips), buffer(2, 2, chips),
-            pltpu.SemaphoreType.DMA((6, 2, 2 * chips)),
+            buffer(chips), buffer(chips, 2), buffer(chips, 2), buffer(chips, 2), buffer(chips, 2),
+            buffer(2), buffer(2), buffer(2, chips, 2),
+            pltpu.SemaphoreType.DMA((5, 2, chips)),
         ],
         compiler_params=pltpu.CompilerParams(collective_id=0, has_side_effects=True),
         name="filter_rotate",

time: 66.4 us -> 62.6 us (0.943); the launches traced: 66.3 us -> 61.3 us
  Pallas kernels: 62.8 us -> 58.8 us
  local copies, waits for them, and re-layouts: 2.22 us -> 1.28 us
    pallas_call x1, Pallas kernels: 62.8 us -> 58.8 us  [filter_and_rotate(): pl.pallas_call(lambda *refs: filter_kernel(width, *refs), out_shape=(pltp...]
    unnamed x4 -> x2, local copies, waits for them, and re-layouts: 2.22 us -> 1.28 us
where the time goes in v4:
time: 62.6 us; the launch traced here: 61.3 us
  Pallas kernels  58.8 us (94%)
  local copies, waits for them, and re-layouts  1.28 us (2%)
  between operations  1.28 us (2%)
    pallas_call x1, Pallas kernels, filter_and_rotate(): pl.pallas_call(lambda *refs: filter_kernel(width, *refs), out_shape=(pltp...  58.8 us
    unnamed x2, local copies, waits for them, and re-layouts  1.28 us

profile of v4, /device:TPU:7, one launch (start us, length us, event | category | flops | bytes accessed | tf_op | source)
XLA Modules:
  0.0 61.3 jit_solution(4778814785094152949)
XLA Ops:
  1.3 58.8 %filter_rotate.1 = (f32[12,16,128]{2,1,0:T(8,128)S(1)}, f32[8,3,8,128]{3,2,1,0:T(8,128)S(1)}) custom-call(bf16[12,16,128]{2,1,0:T(8,128)(2,1)} %bitcast.16, f32[12,16,128]{2,1,0:T(8,128)} %bitcast.15, s32[1]{0:T(128)S(6)} %copy.13.refs_2_, s32[4]{0:T(128)} %refs_3_.1, bf16[1,4]{1,0:T(2,128)(2,1)} %bitcast.17, bf16[256,256]{1,0:T(8,128)(2,1)} %constant.4.clone.refs_5_, ...), custom_call_target="tpu_custom_call" | custom-call | tf_op jit(solution)/shard_map/filter_rotate/pallas_call | solution.py:341
  60.0 0.6 %copy.11 = f32[1,16,12,128]{3,1,2,0:T(8,128)} copy(f32[1,16,12,128]{3,1,2,0:T(8,128)S(1)} %bitcast.14) | data formatting | bytes 196608
  60.7 0.6 %copy.12 = f32[1,16,12,128]{3,1,2,0:T(8,128)} copy(f32[1,16,12,128]{3,1,2,0:T(8,128)S(1)} %bitcast.13) | data formatting | bytes 196608

commit v5 on v4

--- a/solution.py
+++ b/solution.py
@@ -68,7 +68,20 @@
     chips = lax.axis_size("orb") // 4
     z, pair, core = seat()
     return [at(z, pair, 1 - core), at(z, 1 - pair, core)] + [
-        at(lax.rem(z + step, chips), pair, core) for step in by_distance(chips)]
+        at(lax.rem(z + step, chips), pair, core) for step in by_distance(chips) if step in (1, chips - 1)]
+
+
+def vouch(hop, sems):
+    chips = lax.axis_size("orb") // 4
+    z, pair, core = seat()
+    for way, most in ((1, chips // 2 - 1), (chips - 1, (chips - 1) // 2 - 1)):
+        side = 0 if way == 1 else 1
+        if 2 <= hop <= most + 1:
+            pl.semaphore_wait(sems.at[side, hop - 2], 1)
+        if hop <= most:
+            pl.semaphore_signal(
+                sems.at[side, hop - 1], inc=1, device_id=at(lax.rem(z + way, chips), pair, core),
+                device_id_type=MESH)
 
 
 def rotate(filtered, owner_ref, rot_ref, rotated_ref, own, give, got_core, give_z, got_z, give_pair,
@@ -167,9 +180,10 @@
     to_across().wait_send()
 
 
-def filter_kernel(width, orb_ref, pot_ref, degree_ref, owner_ref, rot_ref, ymat_ref, pmat_ref,
+def filter_kernel(width, orb_hbm, pot_hbm, degree_ref, owner_ref, rot_ref, ymat_hbm, pmat_hbm,
                   out_ref, rotated_ref, field, inner, diag, send_sem, recv_sem, pot_send, pot_recv,
-                  hand_send, hand_recv, go_sem, *rotation_scratch):
+                  hand_send, hand_recv, go_sem, vouch_sem, load_sem, orb_ref, pot_ref, ymat_ref,
+                  pmat_ref, *rotation_scratch):
     count = lax.axis_size("dom")
     me = lax.axis_index("dom")
     has_left = me > 0
@@ -217,7 +231,15 @@
     barrier = pltpu.get_barrier_semaphore()
     for peer in peers:
         pl.semaphore_signal(barrier, inc=1, device_id=peer, device_id_type=MESH)
+    loads = [
+        pltpu.make_async_copy(src, dst, load_sem.at[slot])
+        for slot, (src, dst) in enumerate((
+            (orb_hbm, orb_ref), (pot_hbm, pot_ref), (ymat_hbm, ymat_ref), (pmat_hbm, pmat_ref)))]
+    for load in loads:
+        load.start()
+    loads[0].wait()
     field[0, w:2 * w] = orb_ref[...].astype(jnp.float32)
+    loads[1].wait()
     pl.semaphore_wait(barrier, len(peers))
 
     def start(r):
@@ -258,6 +280,8 @@
         diag[half + w:2 * half + w] = jnp.zeros((half,) + diag.shape[1:], jnp.float32)
 
     diag[half:half + w] = pot_ref[...]
+    loads[2].wait()
+    loads[3].wait()
 
     @pl.when(is_second)
     def _():
@@ -314,6 +338,7 @@
         if r + 1 < ROUNDS:
             field[r + 1, w:2 * w] = advanced
             start(r + 1)
+        vouch(r + 1, vouch_sem)
         before = out_ref[...] if r > 0 else jnp.zeros_like(advanced)
         before = jnp.where(degree == 2 * r + 1, inner[half:half + w], before)
         out_ref[...] = jnp.where(degree == 2 * r + 2, advanced, before)
@@ -337,6 +362,7 @@
     ymat, pmat = stencil_matrices(planes, cells, RADIUS)
     vmem = pl.BlockSpec(memory_space=pltpu.VMEM)
     smem = pl.BlockSpec(memory_space=pltpu.SMEM)
+    hbm = pl.BlockSpec(memory_space=pl.ANY)
     buffer = lambda *lead: pltpu.VMEM(lead + piece, jnp.float32)
     filtered, rotated = pl.pallas_call(
         lambda *refs: filter_kernel(width, *refs),
@@ -344,7 +370,7 @@
             pltpu.VMEM(orbitals.shape, jnp.float32),
             pltpu.VMEM((chips,) + piece, jnp.float32),
         ),
-        in_specs=[vmem, vmem, smem, smem, vmem, vmem, vmem],
+        in_specs=[hbm, hbm, smem, smem, vmem, hbm, hbm],
         out_specs=(vmem, vmem),
         scratch_shapes=[
             pltpu.VMEM((ROUNDS, 3 * width, planes, cells), jnp.float32),
@@ -357,6 +383,12 @@
             pltpu.SemaphoreType.DMA((2,)),
             pltpu.SemaphoreType.DMA((2,)),
             pltpu.SemaphoreType.REGULAR,
+            pltpu.SemaphoreType.REGULAR((2, ROUNDS)),
+            pltpu.SemaphoreType.DMA((4,)),
+            pltpu.VMEM(orbitals.shape, orbitals.dtype),
+            pltpu.VMEM(potential.shape, jnp.float32),
+            pltpu.VMEM(ymat.shape, jnp.bfloat16),
+            pltpu.VMEM(pmat.shape, jnp.bfloat16),
             buffer(chips), buffer(chips, 2), buffer(chips, 2), buffer(chips, 2), buffer(chips, 2),
             buffer(2), buffer(2), buffer(2, chips, 2),
             pltpu.SemaphoreType.DMA((5, 2, chips)),

time: 62.6 us -> 62 us (level)
  the two profiles are of different devices: /device:TPU:7 before, /device:TPU:3 now
where the time goes in v5:
time: 62 us; the launch traced here: 61.8 us
  Pallas kernels  59.2 us (95%)
  local copies, waits for them, and re-layouts  1.28 us (2%)
  between operations  1.28 us (2%)
    pallas_call x1, Pallas kernels, filter_and_rotate(): pl.pallas_call(lambda *refs: filter_kernel(width, *refs), out_shape=(pltp...  59.2 us
    unnamed x2, local copies, waits for them, and re-layouts  1.28 us

profile of v5, /device:TPU:3, one launch (start us, length us, event | category | flops | bytes accessed | tf_op | source)
XLA Modules:
  0.0 61.8 jit_solution(6779715702729540987)
XLA Ops:
  1.3 59.2 %filter_rotate.1 = (f32[12,16,128]{2,1,0:T(8,128)S(1)}, f32[8,3,8,128]{3,2,1,0:T(8,128)S(1)}) custom-call(bf16[12,16,128]{2,1,0:T(8,128)(2,1)} %bitcast.16, f32[12,16,128]{2,1,0:T(8,128)} %bitcast.15, s32[1]{0:T(128)S(6)} %copy.13.refs_2_, s32[4]{0:T(128)} %refs_3_.1, bf16[1,4]{1,0:T(2,128)(2,1)} %bitcast.17, bf16[256,256]{1,0:T(8,128)(2,1)} %constant.4.clone.refs_5_, ...), custom_call_target="tpu_custom_call" | custom-call | tf_op jit(solution)/shard_map/filter_rotate/pallas_call | solution.py:367
  60.5 0.6 %copy.11 = f32[1,16,12,128]{3,1,2,0:T(8,128)} copy(f32[1,16,12,128]{3,1,2,0:T(8,128)S(1)} %bitcast.14) | data formatting | bytes 196608
  61.2 0.6 %copy.12 = f32[1,16,12,128]{3,1,2,0:T(8,128)} copy(f32[1,16,12,128]{3,1,2,0:T(8,128)S(1)} %bitcast.13) | data formatting | bytes 196608

commit v6 on v5

--- a/solution.py
+++ b/solution.py
@@ -181,7 +181,7 @@
 
 
 def filter_kernel(width, orb_hbm, pot_hbm, degree_ref, owner_ref, rot_ref, ymat_hbm, pmat_hbm,
-                  out_ref, rotated_ref, field, inner, diag, send_sem, recv_sem, pot_send, pot_recv,
+                  result_ref, out_ref, field, inner, diag, send_sem, recv_sem, pot_send, pot_recv,
                   hand_send, hand_recv, go_sem, vouch_sem, load_sem, orb_ref, pot_ref, ymat_ref,
                   pmat_ref, *rotation_scratch):
     count = lax.axis_size("dom")
@@ -343,7 +343,8 @@
         before = jnp.where(degree == 2 * r + 1, inner[half:half + w], before)
         out_ref[...] = jnp.where(degree == 2 * r + 2, advanced, before)
 
-    rotate(out_ref[...], owner_ref, rot_ref, rotated_ref, *rotation_scratch)
+    result_ref[0] = out_ref[...].reshape(result_ref.shape[1:])
+    rotate(out_ref[...], owner_ref, rot_ref, result_ref.at[1], *rotation_scratch)
 
     for r in range(1, ROUNDS):
         sent(r)
@@ -364,15 +365,13 @@
     smem = pl.BlockSpec(memory_space=pltpu.SMEM)
     hbm = pl.BlockSpec(memory_space=pl.ANY)
     buffer = lambda *lead: pltpu.VMEM(lead + piece, jnp.float32)
-    filtered, rotated = pl.pallas_call(
+    result = pl.pallas_call(
         lambda *refs: filter_kernel(width, *refs),
-        out_shape=(
+        out_shape=pltpu.VMEM((2, chips) + piece, jnp.float32),
+        in_specs=[hbm, hbm, smem, smem, vmem, hbm, hbm],
+        out_specs=vmem,
+        scratch_shapes=[
             pltpu.VMEM(orbitals.shape, jnp.float32),
-            pltpu.VMEM((chips,) + piece, jnp.float32),
-        ),
-        in_specs=[hbm, hbm, smem, smem, vmem, hbm, hbm],
-        out_specs=(vmem, vmem),
-        scratch_shapes=[
             pltpu.VMEM((ROUNDS, 3 * width, planes, cells), jnp.float32),
             pltpu.VMEM((2 * width, planes, cells), jnp.float32),
             pltpu.VMEM((width + 2 * RADIUS, planes, cells), jnp.float32),
@@ -396,7 +395,8 @@
         compiler_params=pltpu.CompilerParams(collective_id=0, has_side_effects=True),
         name="filter_rotate",
     )(orbitals, potential, degree, owners, coefficients, jnp.asarray(ymat), jnp.asarray(pmat))
-    return filtered, rotated.reshape(orbitals.shape)
+    result = result.reshape((2,) + orbitals.shape)
+    return result[0], result[1]
 
 
 def per_device(orbitals, potential, degree, owners, rotation):

time: 62 us -> 61.4 us (level)
    unnamed x2 -> x0, local copies, waits for them, and re-layouts: 1.28 us -> none
    slice x0 -> x1, local copies, waits for them, and re-layouts: none -> 0.69 us  [filter_and_rotate(): return (result[0], result[1])]
where the time goes in v6:
time: 61.4 us; the launch traced here: 61.2 us
  Pallas kernels  59.3 us (97%)
  between operations  1.28 us (2%)
  local copies, waits for them, and re-layouts  0.69 us (1%)
    pallas_call x1, Pallas kernels, filter_and_rotate(): pl.pallas_call(lambda *refs: filter_kernel(width, *refs), out_shape=pltpu...  59.3 us

profile of v6, /device:TPU:3, one launch (start us, length us, event | category | flops | bytes accessed | tf_op | source)
XLA Modules:
  0.0 61.2 jit_solution(15389431380603465864)
XLA Ops:
  1.3 59.3 %filter_rotate.1 = f32[2,8,3,8,128]{4,3,2,1,0:T(8,128)S(1)} custom-call(bf16[12,16,128]{2,1,0:T(8,128)(2,1)} %bitcast.18, f32[12,16,128]{2,1,0:T(8,128)} %bitcast.17, s32[1]{0:T(128)S(6)} %copy.9.refs_2_, s32[4]{0:T(128)} %refs_3_.1, bf16[1,4]{1,0:T(2,128)(2,1)} %bitcast.19, bf16[256,256]{1,0:T(8,128)(2,1)} %constant.4.clone.refs_5_, ...), custom_call_target="tpu_custom_call" | custom-call | tf_op jit(solution)/shard_map/filter_rotate/pallas_call | solution.py:368
  60.5 0.7 %fusion = (f32[1,8,3,8,128]{4,3,2,1,0:T(8,128)}, f32[1,8,3,8,128]{4,3,2,1,0:T(8,128)}) fusion(f32[2,8,3,8,128]{4,3,2,1,0:T(8,128)S(1)} %filter_rotate.1), kind=kLoop, calls=%fused_computation | loop fusion | bytes 393216 | tf_op jit(solution)/shard_map/slice | solution.py:399

commit v7 on v6

--- a/solution.py
+++ b/solution.py
@@ -108,8 +108,8 @@
     def scattered(k):
         return copy(1, give_z.at[k], got_z.at[k], k, at(k, pair, core))
 
-    def to_across():
-        return copy(2, give_pair, got_pair, 0, across)
+    def to_across(which):
+        return copy(2, give_pair.at[which], got_pair.at[which], which, across)
 
     def gather(k):
         piece = panels.at[core, z]
@@ -151,13 +151,15 @@
             scatter(k).start()
     for step in near:
         scattered(chunk_of(step)).wait_recv()
-    total = got_z[0]
-    for k in range(1, chips):
-        total = total + got_z[k]
-    give_pair[...] = total
-    to_across().start()
-    to_across().wait_recv()
-    panels[core, z] = give_pair[...] + got_pair[...]
+    for which in range(2):
+        total = got_z[0, which]
+        for k in range(1, chips):
+            total = total + got_z[k, which]
+        give_pair[which] = total
+        to_across(which).start()
+    for which in range(2):
+        to_across(which).wait_recv()
+        panels[core, z, which] = give_pair[which] + got_pair[which]
     for step in near[::-1]:
         gather(chunk_of(step)).start()
     for step in [0] + near:
@@ -177,7 +179,8 @@
             scatter(k).wait_send()
             gather(k).wait_send()
         share(k).wait_send()
-    to_across().wait_send()
+    for which in range(2):
+        to_across(which).wait_send()
 
 
 def filter_kernel(width, orb_hbm, pot_hbm, degree_ref, owner_ref, rot_ref, ymat_hbm, pmat_hbm,

time: 61.4 us -> 61.4 us (level)
  no operation moved by 1% of the time
where the time goes in v7:
time: 61.4 us; the launch traced here: 61.2 us
  Pallas kernels  59.3 us (97%)
  between operations  1.28 us (2%)
  local copies, waits for them, and re-layouts  0.69 us (1%)
    pallas_call x1, Pallas kernels, filter_and_rotate(): pl.pallas_call(lambda *refs: filter_kernel(width, *refs), out_shape=pltpu...  59.3 us

profile of v7, /device:TPU:3, one launch (start us, length us, event | category | flops | bytes accessed | tf_op | source)
XLA Modules:
  0.0 61.2 jit_solution(11613212161372693310)
XLA Ops:
  1.3 59.3 %filter_rotate.1 = f32[2,8,3,8,128]{4,3,2,1,0:T(8,128)S(1)} custom-call(bf16[12,16,128]{2,1,0:T(8,128)(2,1)} %bitcast.18, f32[12,16,128]{2,1,0:T(8,128)} %bitcast.17, s32[1]{0:T(128)S(6)} %copy.9.refs_2_, s32[4]{0:T(128)} %refs_3_.1, bf16[1,4]{1,0:T(2,128)(2,1)} %bitcast.19, bf16[256,256]{1,0:T(8,128)(2,1)} %constant.4.clone.refs_5_, ...), custom_call_target="tpu_custom_call" | custom-call | tf_op jit(solution)/shard_map/filter_rotate/pallas_call | solution.py:371
  60.5 0.7 %fusion = (f32[1,8,3,8,128]{4,3,2,1,0:T(8,128)}, f32[1,8,3,8,128]{4,3,2,1,0:T(8,128)}) fusion(f32[2,8,3,8,128]{4,3,2,1,0:T(8,128)S(1)} %filter_rotate.1), kind=kLoop, calls=%fused_computation | loop fusion | bytes 393216 | tf_op jit(solution)/shard_map/slice | solution.py:402
